TPU v7x, 128 devices: a whole 4x4x4 slice. The times are simulated.
128 devices in a mesh: row: 8 (over x, y_hi), col: 16 (over y_lo, z, core).
Axes of the slice: x: 4, y: 4 (y_hi: 2, y_lo: 2; y = y_hi * 2 + y_lo), z: 4, core: 2. Of those that a mesh axis runs over, the one named last changes fastest.
Arguments:
- front_trailing: float32 [16384, 16384], P('row', 'col'), may hold values from -6 to 6
- panel_columns: float32 [16384, 1024], P('row', 'col'), may hold values from -0.1875 to 0.1875
- panel_rows: float32 [1024, 16384], P('row', 'col'), may hold values from -6 to 6
- pivots: int32 [1024], replicated, may hold values from 0 to 1023, each once
- diag_inverse: float32 [1024, 1024], replicated, may hold values from -0.1875 to 0.1875
- test_matrix: float32 [16384, 512], P('col'), may hold values from -0.046875 to 0.046875
Outputs:
- schur: float32 [16384, 16384], P('row', 'col')
- off_samples: float32 [16384, 512], P(('row', 'col'))
- leaf_blocks: float32 [16384, 128], P(('row', 'col'))
- group_gram: float32 [8, 512, 512], P('row')
Inputs may be any that keep to these rules, and one draw needn't show every extreme that they name: pivots names each of 0 to 1023 once.
All inputs are finite; a program needn't handle non-finite values.
Results may differ from a plain program's by a relative error of at most 0.000084.
Values sent between devices are 32-bit elements; how exact they have to be, the bound alone decides.
A program may use at most 128 MiB of HBM per device.

v0:
```python
import jax
import jax.numpy as jnp
from jax import lax
from jax.sharding import PartitionSpec as P

LEAF = 128


def swapped(block, axis, apart):
    count = lax.axis_size(axis)
    route = []
    for low in range(count):
        high = low | 1 << apart
        if high != low and high < count:
            route += [(low, high), (high, low)]
    return lax.ppermute(block, axis, route)


def from_root(block, axis, source):
    block = jnp.where(lax.axis_index(axis) == source, block, jnp.zeros_like(block))
    return lax.psum(block, axis)


def product(left, right):
    return jnp.dot(left, right, precision=lax.Precision.HIGHEST, preferred_element_type=jnp.float32)


def inner_gram(samples_local):
    return lax.dot_general(
        samples_local,
        samples_local,
        (((0,), (0,)), ((), ())),
        precision=lax.Precision.HIGHEST,
        preferred_element_type=jnp.float32,
    )


def body(front_trailing, panel_columns, panel_rows, pivots, diag_inverse, test_matrix):
    row_count = lax.axis_size("row")
    col_count = lax.axis_size("col")
    row_index = lax.axis_index("row")
    col_index = lax.axis_index("col")
    height, width = front_trailing.shape
    upper_full = lax.all_gather(panel_rows, "row", axis=0, tiled=True)
    upper = jnp.take(upper_full, pivots, axis=0)
    lower = product(lax.all_gather(panel_columns, "col", axis=1, tiled=True), diag_inverse)
    update = product(lower, upper)
    schur = front_trailing - update
    global_rows = row_index * height + jnp.arange(height, dtype=jnp.int32)
    global_cols = col_index * width + jnp.arange(width, dtype=jnp.int32)
    same_leaf = global_rows[:, None] // LEAF == global_cols[None, :] // LEAF
    masked = jnp.where(same_leaf, jnp.zeros_like(schur), schur)
    per_device = height // col_count
    summed = lax.psum(product(masked, test_matrix), "col")
    own_samples = lax.dynamic_slice_in_dim(summed, col_index * per_device, per_device, 0)
    gram = inner_gram(summed)
    partner = swapped(gram, "row", 0)
    group_gram = ((gram + partner) / (2 * height))[None]
    ratio = col_count // row_count
    blocks_count = width // LEAF
    region_start = col_index % ratio * width
    region = lax.dynamic_slice_in_dim(schur, region_start, width, 0)
    candidates = jnp.diagonal(
        region.reshape(blocks_count, LEAF, blocks_count, LEAF), axis1=0, axis2=2
    )
    candidates = jnp.moveaxis(candidates, -1, 0)
    received = [from_root(candidates, "col", row_index * ratio + source) for source in range(ratio)]
    stacked = jnp.stack(received).reshape(ratio * blocks_count, LEAF, LEAF)
    first_row = col_index * per_device
    picked = lax.dynamic_slice_in_dim(stacked, first_row // LEAF, per_device // LEAF, 0)
    leaf_blocks = picked.reshape(per_device, LEAF)
    return (schur, own_samples, leaf_blocks, group_gram)


def solution(mesh):
    placed = (P("row", "col"), P("row", "col"), P("row", "col"), P(), P(), P("col", None))
    return jax.shard_map(
        body,
        mesh=mesh,
        in_specs=placed,
        out_specs=(
            P("row", "col"),
            P(("row", "col"), None),
            P(("row", "col"), None),
            P("row", None, None),
        ),
        check_vma=False,
    )
```

profile of v0, /device:TPU:0, one launch (start us, length us, event | category | flops | bytes accessed | tf_op | source)
XLA Modules:
  0.0 403.2 jit_solution(12109506079082405454)
XLA Ops:
  7.2 0.0 copy-start
  7.2 0.0 all-gather.5.cloned.1.call-start
  7.2 0.7 all-gather.5.cloned.1.call-update
  7.9 0.0 all-gather.3.cloned.1.call-start
  8.0 0.7 all-gather.3.cloned.1.call-update
  8.7 0.0 all-reduce.3.cloned.1.call-start
  8.8 0.7 compare_and_fusion
  9.5 0.7 fusion.19
  10.2 74.2 %all-gather.5.cloned.1.call-done = f32[1024,1024]{1,0:T(8,128)} async-done(((f32[128,1024]{1,0:T(8,128)}), f32[1024,1024]{1,0:T(8,128)}) %all-gather.5.cloned.1.call-update) | async-done | bytes 4194320 | tf_op jit(solution)/shard_map/all_gather | solution.py:44
  84.4 8.5 %gather_fusion = f32[1024,1024]{1,0:T(8,128)} fusion(f32[1024,1024]{1,0:T(8,128)} %all-gather.5.cloned.1.call-done, s32[1024]{0:T(1024)S(1)} %fusion.19), kind=kCustom, calls=%fused_computation | custom fusion | bytes 8392704 | tf_op jit(solution)/shard_map/jit(_take)/gather | solution.py:45
  92.9 43.2 %all-gather.3.cloned.1.call-done = f32[2048,1024]{0,1:T(8,128)} async-done(((f32[2048,64]{0,1:T(8,128)}), f32[2048,1024]{0,1:T(8,128)}) %all-gather.3.cloned.1.call-update) | async-done | bytes 8388624 | tf_op jit(solution)/shard_map/all_gather | solution.py:46
  136.1 0.0 copy-start.1
  136.1 0.0 copy-start.3
  136.1 30.1 %fusion.22 = f32[2048,1024]{1,0:T(8,128)S(1)} fusion(f32[2048,1024]{0,1:T(8,128)} %all-gather.3.cloned.1.call-done, f32[1024,1024]{1,0:T(8,128)} %param.10), kind=kOutput, calls=%fused_computation.45 | convolution fusion | flops 25769803776 | bytes 20971520 | tf_op jit(solution)/shard_map/dot_general | solution.py:25
  166.2 0.0 copy-done.1
  166.2 0.0 copy-done.3
  166.2 29.4 %fusion.8 = f32[2048,1024]{1,0:T(8,128)S(1)} fusion(f32[2048,1024]{1,0:T(8,128)S(1)} %copy-done.3, f32[2048,1024]{1,0:T(8,128)S(1)} %fusion.22, f32[1024,1024]{1,0:T(8,128)S(1)} %copy-done.1, pred[1024]{0:T(1024)(128)(4,1)S(1)} %compare_and_fusion), kind=kOutput, calls=%fused_computation.12 | convolution fusion | flops 25772949504 | bytes 29361152 | tf_op jit(solution)/shard_map/dot_general | solution.py:25
  195.7 0.0 copy-start.2
  195.7 0.3 dynamic-slice_bitcast_fusion
  196.0 3.1 copy-done.2
  199.1 1.0 copy.12
  200.1 2.7 copy.14
  202.8 2.8 gather_fusion.1
  205.6 0.0 copy-done
  205.6 17.4 %fusion = f32[2048,512]{1,0:T(8,128)} fusion(f32[1024,512]{1,0:T(8,128)S(1)} %copy-done, f32[2048,1024]{1,0:T(8,128)} %copy-done.2, s32[1024]{0:T(1024)S(1)} %add_select_fusion.1, s32[2048]{0:T(1024)S(1)} %add_select_fusion), kind=kOutput, calls=%fused_computation.2 | convolution fusion | flops 12889096192 | bytes 14692352 | tf_op jit(solution)/shard_map/dot_general | solution.py:25
  222.9 1.1 select_bitcast_fusion.1
  224.0 0.0 all-reduce.3.cloned.1.call-update
  224.0 134.5 %all-reduce.3.cloned.1.call-done = (f32[2048,512]{1,0:T(8,128)}, f32[1,8,128,128]{3,2,1,0:T(8,128)}, f32[1,8,128,128]{3,2,1,0:T(8,128)}) async-done(((f32[2048,512]{1,0:T(8,128)}, f32[1,8,128,128]{3,2,1,0:T(8,128)}, f32[1,8,128,128]{3,2,1,0:T(8,128)}), (f32[2048,512]{1,0:T(8,128)}, f32[1,8,128,128]{3,2,1,0:T(8,128)}, f32[1,8,128,128]{3,2,1,0:T(8,128)})) %all-reduce.3.cloned.1.call-update) | async-done | bytes 5242896 | tf_op jit(solution)/shard_map/psum | solution.py:54
  358.5 10.2 %fusion.23 = f32[512,512]{1,0:T(8,128)S(1)} fusion(f32[2048,512]{1,0:T(8,128)} %get-tuple-element.4), kind=kOutput, calls=%fused_computation.46 | convolution fusion | flops 6442450944 | bytes 5242880 | tf_op jit(solution)/shard_map/dot_general | solution.py:29
  368.7 2.8 collective-permute-start
  371.5 1.3 pad_maximum_fusion
  372.8 0.6 dynamic-slice_bitcast_fusion.1
  373.4 1.7 constant_dynamic-slice_fusion
  375.1 19.2 %collective-permute-done = f32[512,512]{1,0:T(8,128)} collective-permute-done((f32[512,512]{1,0:T(8,128)S(1)}, f32[512,512]{1,0:T(8,128)}, u32[]{:S(2)}, u32[]{:S(2)}) %collective-permute-start) | collective-permute-done | bytes 1048608 | tf_op jit(solution)/shard_map/ppermute | solution.py:16
  394.2 2.4 multiply_bitcast_fusion
  (3 shorter events, 0.0 us)
Async XLA Ops:
  7.2 198.4 %copy-start = (f32[1024,512]{1,0:T(8,128)S(1)}, f32[1024,512]{1,0:T(8,128)}, u32[]{:S(2)}) copy-start(f32[1024,512]{1,0:T(8,128)} %param.11) | copy-start | bytes 6291460
  7.2 77.2 %all-gather.5.cloned.1.call-start = ((), (), s32[]{:S(2)}) async-start(), calls=%async_computation.1 | async-start | bytes 4718592 | tf_op jit(solution)/shard_map/all_gather | solution.py:44
  7.9 128.2 %all-gather.3.cloned.1.call-start = ((), (), s32[]{:S(2)}) async-start(), calls=%async_computation | async-start | bytes 8912896 | tf_op jit(solution)/shard_map/all_gather | solution.py:46
  8.7 349.8 %all-reduce.3.cloned.1.call-start = ((), (), s32[]{:S(2)}) async-start(), calls=%async_computation.2 | async-start | bytes 10485760 | tf_op jit(solution)/shard_map/psum | solution.py:54
  136.1 30.1 %copy-start.1 = (f32[1024,1024]{1,0:T(8,128)S(1)}, f32[1024,1024]{1,0:T(8,128)}, u32[]{:S(2)}) copy-start(f32[1024,1024]{1,0:T(8,128)} %gather_fusion) | copy-start | bytes 12582916
  136.1 30.1 %copy-start.3 = (f32[2048,1024]{1,0:T(8,128)S(1)}, f32[2048,1024]{1,0:T(8,128)}, u32[]{:S(2)}) copy-start(f32[2048,1024]{1,0:T(8,128)} %param.6) | copy-start | bytes 25165828
  195.7 3.4 copy-start.2
  368.7 25.6 %collective-permute-start = (f32[512,512]{1,0:T(8,128)S(1)}, f32[512,512]{1,0:T(8,128)}, u32[]{:S(2)}, u32[]{:S(2)}) collective-permute-start(f32[512,512]{1,0:T(8,128)S(1)} %fusion.23), channel_id=1, source_target_pairs={{0,16},{16,0},{32,48},{48,32},{64,80},{80,64},{96,112},{112,96},{1... | collective-permute-start | bytes 3145736 | tf_op jit(solution)/shard_map/ppermute | solution.py:16
Sparse Core Ops, SparseCore 0:
  10.3 74.0 all-gather.4
  86.1 49.9 all-gather.2
  224.1 134.3 all-reduce.2
where the time goes:
time: 404 us; the launch traced here: 403 us
  waiting for transfers between devices  272 us (67%)
  matrix products  87 us (22%)
  local copies, waits for them, and re-layouts  20.7 us (5%)
  between operations  13.9 us (3%)
  other arithmetic  6.2 us (2%)
    psum x1, waiting for transfers between devices, body(): summed = lax.psum(product(masked, test_matrix), 'col')  134 us
    dot_general x3, matrix products, product(): jnp.dot(left, right, precision=lax.Precision.HIGHEST, preferred_element_t...  76.9 us
    all_gather x1, waiting for transfers between devices, body(): upper_full = lax.all_gather(panel_rows, 'row', axis=0, tiled=True)  74.2 us
    all_gather x1, waiting for transfers between devices, body(): lax.all_gather(panel_columns, 'col', axis=1, tiled=True)  43.2 us
    ppermute x1, waiting for transfers between devices, swapped(): return lax.ppermute(block, axis, route)  19.2 us
    dot_general x1, matrix products, inner_gram(): lax.dot_general(samples_local, samples_local, (((0,), (0,)), ((), ())), p...  10.2 us
    gather x1, local copies, waits for them, and re-layouts, body(): upper = jnp.take(upper_full, pivots, axis=0)  8.52 us
  transfers between devices with their start and end apart: 4, of which 4 were waited for; matrix products, arithmetic and copies ran while one was open for 3% of the time, Pallas kernels for 0%

commit v1 on v0

--- a/solution.py
+++ b/solution.py
@@ -4,6 +4,13 @@
 from jax.sharding import PartitionSpec as P
 
 LEAF = 128
+
+
+def swapped_in(array, axis, d):
+    count = lax.axis_size(axis)
+    parts = jnp.stack([array for _ in range(count)])
+    parts = lax.all_to_all(parts, axis, split_axis=0, concat_axis=0)
+    return jnp.concatenate(parts, axis=d)
 
 
 def swapped(block, axis, apart):
@@ -41,7 +48,7 @@
     row_index = lax.axis_index("row")
     col_index = lax.axis_index("col")
     height, width = front_trailing.shape
-    upper_full = lax.all_gather(panel_rows, "row", axis=0, tiled=True)
+    upper_full = swapped_in(panel_rows, "row", 0)
     upper = jnp.take(upper_full, pivots, axis=0)
     lower = product(lax.all_gather(panel_columns, "col", axis=1, tiled=True), diag_inverse)
     update = product(lower, upper)

time: 404 us -> 378 us (0.936)
  waiting for transfers between devices: 272 us -> 235 us
  starting transfers between devices: 2.91 us -> 10 us
    all_gather x1 -> x0, waiting for transfers between devices: 74.2 us -> none  [body(): upper_full = lax.all_gather(panel_rows, 'row', axis=0, tiled=True)]
    all_to_all x0 -> x1, waiting for transfers between devices: none -> 59.5 us  [swapped_in(): parts = lax.all_to_all(parts, axis, split_axis=0, concat_axis=0)]
    all_gather x1, waiting for transfers between devices: 43.2 us -> 18.9 us  [body(): lax.all_gather(panel_columns, 'col', axis=1, tiled=True)]
    all_to_all x0 -> x1, starting transfers between devices: none -> 7.17 us  [swapped_in(): parts = lax.all_to_all(parts, axis, split_axis=0, concat_axis=0)]
  transfers between devices with their start and end apart: 4 -> 4, of which waited for: 4 -> 4; matrix products, arithmetic and copies ran while one was open for 3% -> 4% of each run, Pallas kernels for 0% -> 0%
where the time goes in v1:
time: 378 us; the launch traced here: 377 us
  waiting for transfers between devices  235 us (62%)
  matrix products  88.9 us (24%)
  local copies, waits for them, and re-layouts  24.4 us (6%)
  between operations  14.2 us (4%)
  starting transfers between devices  10 us (3%)
  other arithmetic  4.83 us (1%)
    psum x1, waiting for transfers between devices, body(): summed = lax.psum(product(masked, test_matrix), 'col')  137 us
    dot_general x3, matrix products, product(): jnp.dot(left, right, precision=lax.Precision.HIGHEST, preferred_element_t...  78.6 us
    all_to_all x1, waiting for transfers between devices, swapped_in(): parts = lax.all_to_all(parts, axis, split_axis=0, concat_axis=0)  59.5 us
    ppermute x1, waiting for transfers between devices, swapped(): return lax.ppermute(block, axis, route)  19.2 us
    all_gather x1, waiting for transfers between devices, body(): lax.all_gather(panel_columns, 'col', axis=1, tiled=True)  18.9 us
    dot_general x1, matrix products, inner_gram(): lax.dot_general(samples_local, samples_local, (((0,), (0,)), ((), ())), p...  10.2 us
    gather x1, local copies, waits for them, and re-layouts, body(): upper = jnp.take(upper_full, pivots, axis=0)  8.61 us
  transfers between devices with their start and end apart: 4, of which 4 were waited for; matrix products, arithmetic and copies ran while one was open for 4% of the time, Pallas kernels for 0%

profile of v1, /device:TPU:0, one launch (start us, length us, event | category | flops | bytes accessed | tf_op | source)
XLA Modules:
  0.0 377.1 jit_solution(5725426877560470006)
XLA Ops:
  7.2 0.0 copy-start
  7.2 0.0 all-gather.2.cloned.1.call-start
  7.2 0.7 all-gather.2.cloned.1.call-update
  7.9 3.6 stack.8
  11.5 0.0 copy-start.3
  11.5 7.2 %all-to-all-start = ((f32[8,128,1024]{2,1,0:T(8,128)}), f32[8,128,1024]{2,1,0:T(8,128)}, u32[]{:S(2)}, u32[]{:S(2)}) async-start(f32[8,128,1024]{2,1,0:T(8,128)} %stack.8), calls=%async_computation | async-start | bytes 8388608 | tf_op jit(solution)/shard_map/all_to_all | solution.py:12
  18.7 0.0 all-reduce.3.cloned.1.call-start
  18.8 0.0 copy-done.3
  18.8 59.5 %all-to-all-done = f32[8,128,1024]{2,1,0:T(8,128)} async-done(((f32[8,128,1024]{2,1,0:T(8,128)}), f32[8,128,1024]{2,1,0:T(8,128)}, u32[]{:S(2)}, u32[]{:S(2)}) %all-to-all-start) | async-done | bytes 4194336 | tf_op jit(solution)/shard_map/all_to_all | solution.py:12
  78.3 8.6 %gather_fusion = f32[1024,1024]{1,0:T(8,128)} fusion(f32[1024,1024]{1,0:T(8,128)} %bitcast, s32[1024]{0:T(1024)S(1)} %fusion.19), kind=kCustom, calls=%fused_computation | custom fusion | bytes 8392704 | tf_op jit(solution)/shard_map/jit(_take)/gather | solution.py:52
  86.9 18.9 %all-gather.2.cloned.1.call-done = f32[2048,1024]{0,1:T(8,128)} async-done(((f32[2048,64]{0,1:T(8,128)}), f32[2048,1024]{0,1:T(8,128)}) %all-gather.2.cloned.1.call-update) | async-done | bytes 8388624 | tf_op jit(solution)/shard_map/all_gather | solution.py:53
  105.8 0.0 copy-start.1
  105.8 30.1 %fusion.22 = f32[2048,1024]{1,0:T(8,128)S(1)} fusion(f32[2048,1024]{0,1:T(8,128)} %all-gather.2.cloned.1.call-done, f32[1024,1024]{1,0:T(8,128)} %param.10), kind=kOutput, calls=%fused_computation.45 | convolution fusion | flops 25769803776 | bytes 20971520 | tf_op jit(solution)/shard_map/dot_general | solution.py:32
  135.9 0.0 copy-done.1
  135.9 31.4 %fusion.8 = f32[2048,1024]{1,0:T(8,128)S(1)} fusion(f32[2048,1024]{1,0:T(8,128)} %param.6, f32[2048,1024]{1,0:T(8,128)S(1)} %fusion.22, f32[1024,1024]{1,0:T(8,128)S(1)} %copy-done.1, pred[1024]{0:T(1024)(128)(4,1)S(1)} %compare_and_fusion), kind=kOutput, calls=%fused_computation.12 | convolution fusion | flops 25772949504 | bytes 29361152 | tf_op jit(solution)/shard_map/dot_general | solution.py:32
  167.3 0.0 copy-start.2
  167.3 0.3 dynamic-slice_bitcast_fusion
  167.7 3.1 copy-done.2
  170.7 1.0 copy.12
  171.7 2.7 copy.14
  174.4 2.8 gather_fusion.1
  177.2 0.0 copy-done
  177.2 17.1 %fusion = f32[2048,512]{1,0:T(8,128)} fusion(f32[1024,512]{1,0:T(8,128)S(1)} %copy-done, f32[2048,1024]{1,0:T(8,128)} %copy-done.2, s32[1024]{0:T(1024)S(1)} %add_select_fusion.1, s32[2048]{0:T(1024)S(1)} %add_select_fusion), kind=kOutput, calls=%fused_computation.2 | convolution fusion | flops 12889096192 | bytes 14692352 | tf_op jit(solution)/shard_map/dot_general | solution.py:32
  194.4 1.1 select_bitcast_fusion.1
  195.4 0.0 all-reduce.3.cloned.1.call-update
  195.5 136.6 %all-reduce.3.cloned.1.call-done = (f32[2048,512]{1,0:T(8,128)}, f32[1,8,128,128]{3,2,1,0:T(8,128)}, f32[1,8,128,128]{3,2,1,0:T(8,128)}) async-done(((f32[2048,512]{1,0:T(8,128)}, f32[1,8,128,128]{3,2,1,0:T(8,128)}, f32[1,8,128,128]{3,2,1,0:T(8,128)}), (f32[2048,512]{1,0:T(8,128)}, f32[1,8,128,128]{3,2,1,0:T(8,128)}, f32[1,8,128,128]{3,2,1,0:T(8,128)})) %all-reduce.3.cloned.1.call-update) | async-done | bytes 5242896 | tf_op jit(solution)/shard_map/psum | solution.py:61
  332.0 10.2 %fusion.23 = f32[512,512]{1,0:T(8,128)S(1)} fusion(f32[2048,512]{1,0:T(8,128)} %get-tuple-element.4), kind=kOutput, calls=%fused_computation.46 | convolution fusion | flops 6442450944 | bytes 5242880 | tf_op jit(solution)/shard_map/dot_general | solution.py:36
  342.3 2.8 collective-permute-start
  345.1 1.3 pad_maximum_fusion
  346.4 0.6 dynamic-slice_bitcast_fusion.1
  347.0 1.7 constant_dynamic-slice_fusion
  348.7 19.2 %collective-permute-done = f32[512,512]{1,0:T(8,128)} collective-permute-done((f32[512,512]{1,0:T(8,128)S(1)}, f32[512,512]{1,0:T(8,128)}, u32[]{:S(2)}, u32[]{:S(2)}) %collective-permute-start) | collective-permute-done | bytes 1048608 | tf_op jit(solution)/shard_map/ppermute | solution.py:23
  367.9 2.4 multiply_bitcast_fusion
  (5 shorter events, 0.0 us)
Async XLA Ops:
  7.2 170.0 %copy-start = (f32[1024,512]{1,0:T(8,128)S(1)}, f32[1024,512]{1,0:T(8,128)}, u32[]{:S(2)}) copy-start(f32[1024,512]{1,0:T(8,128)} %param.11) | copy-start | bytes 6291460
  7.2 98.6 %all-gather.2.cloned.1.call-start = ((), (), s32[]{:S(2)}) async-start(), calls=%async_computation.1 | async-start | bytes 8912896 | tf_op jit(solution)/shard_map/all_gather | solution.py:53
  11.5 7.3 %copy-start.3 = (s32[1024]{0:T(1024)S(1)}, s32[1024]{0:T(1024)}, u32[]{:S(2)}) copy-start(s32[1024]{0:T(1024)} %param.9) | copy-start | bytes 12292
  11.5 66.8 %all-to-all-start = ((f32[8,128,1024]{2,1,0:T(8,128)}), f32[8,128,1024]{2,1,0:T(8,128)}, u32[]{:S(2)}, u32[]{:S(2)}) async-start(f32[8,128,1024]{2,1,0:T(8,128)} %stack.8), calls=%async_computation | async-start | bytes 8388608 | tf_op jit(solution)/shard_map/all_to_all | solution.py:12
  18.7 313.4 %all-reduce.3.cloned.1.call-start = ((), (), s32[]{:S(2)}) async-start(), calls=%async_computation.2 | async-start | bytes 10485760 | tf_op jit(solution)/shard_map/psum | solution.py:61
  105.8 30.1 %copy-start.1 = (f32[1024,1024]{1,0:T(8,128)S(1)}, f32[1024,1024]{1,0:T(8,128)}, u32[]{:S(2)}) copy-start(f32[1024,1024]{1,0:T(8,128)} %gather_fusion) | copy-start | bytes 12582916
  167.3 3.4 copy-start.2
  342.3 25.6 %collective-permute-start = (f32[512,512]{1,0:T(8,128)S(1)}, f32[512,512]{1,0:T(8,128)}, u32[]{:S(2)}, u32[]{:S(2)}) collective-permute-start(f32[512,512]{1,0:T(8,128)S(1)} %fusion.23), channel_id=1, source_target_pairs={{0,16},{16,0},{32,48},{48,32},{64,80},{80,64},{96,112},{112,96},{1... | collective-permute-start | bytes 3145736 | tf_op jit(solution)/shard_map/ppermute | solution.py:23
Sparse Core Ops, SparseCore 0:
  9.7 96.0 all-gather.1
  195.6 136.4 all-reduce.2
